TPU v7x, 32 devices: a whole 2x2x4 slice. The times are simulated.
32 devices in a mesh: gx: 4 (over z), gy: 8 (over y, x, core).
Axes of the slice: x: 2, y: 2, z: 4, core: 2. Of those that a mesh axis runs over, the one named last changes fastest.
Arguments:
- basis: float32 [20, 3, 32, 64, 512], P(None, None, 'gx', 'gy'), may hold values from -8 to 8
- base_flow: float32 [3, 32, 64, 512], P(None, 'gx', 'gy'), may hold values from -6 to 6
Outputs:
- next_vector: float32 [3, 32, 64, 512], P(None, 'gx', 'gy')
- hessenberg: float32 [21], replicated
All inputs are finite; a program needn't handle non-finite values.
Results may differ from a plain program's by a relative error of at most 0.005.
Values sent between devices are 32-bit elements; how exact they have to be, the bound alone decides.
A program may use at most 128 MiB of HBM per device.

v0:
```python
import functools
import math

import jax
import jax.numpy as jnp
import numpy as np
from jax import lax
from jax.experimental import pallas as pl
from jax.experimental.pallas import tpu as pltpu
from jax.sharding import PartitionSpec as P

SWEEPS = 4
time_step = 0.02
viscosity = 0.05
pressure_shift = 0.25
relaxation = 0.6
coarse_face = 2.0
coarse_reach = 4.0
norm_eps = 1e-06
inner_a = 0.8717401485096066
inner_b = 0.5917001814331423
inner_c = 0.2092992179024789
MESH = pl.DeviceIdType.MESH
DIRS = [(dx, dy) for dx in (-1, 0, 1) for dy in (-1, 0, 1) if (dx, dy) != (0, 0)]


def legendre_seven(points):
    before = points * 0.0 + 1.0
    current = points.copy()
    for degree in range(1, 7):
        following = ((2 * degree + 1) * points * current - degree * before) / (degree + 1)
        before = current
        current = following
    return current


def jacobi_eigen(matrix):
    work = matrix.copy()
    vectors = np.eye(8)
    for sweep_idx in range(10):
        for p_idx in range(7):
            for q_idx in range(p_idx + 1, 8):
                off_value = float(work[p_idx, q_idx])
                if abs(off_value) > 1e-300:
                    theta = 0.5 * math.atan2(
                        2.0 * off_value, float(work[p_idx, p_idx] - work[q_idx, q_idx])
                    )
                    cosine = math.cos(theta)
                    sine = math.sin(theta)
                    rotation = np.eye(8)
                    rotation[p_idx, p_idx] = cosine
                    rotation[q_idx, q_idx] = cosine
                    rotation[q_idx, p_idx] = sine
                    rotation[p_idx, q_idx] = -sine
                    work = rotation.T @ work @ rotation
                    vectors = vectors @ rotation
    eigenvalues = np.array([work[row_idx, row_idx] for row_idx in range(8)])
    return (eigenvalues, vectors)


def gll_tables():
    order = 7
    nodes = np.array([-1.0, -inner_a, -inner_b, -inner_c, inner_c, inner_b, inner_a, 1.0])
    node_values = legendre_seven(nodes)
    weights = 2.0 / (order * (order + 1) * node_values**2)
    derivative = np.zeros((8, 8))
    for row_idx in range(8):
        for col_idx in range(8):
            if row_idx != col_idx:
                derivative[row_idx, col_idx] = node_values[row_idx] / (
                    node_values[col_idx] * (nodes[row_idx] - nodes[col_idx])
                )
    derivative[0, 0] = -order * (order + 1) / 4.0
    derivative[7, 7] = order * (order + 1) / 4.0
    stiffness = derivative.T @ (weights[:, None] * derivative)
    scaling = 1.0 / np.sqrt(weights)
    symmetric = scaling[:, None] * stiffness * scaling[None, :]
    symmetric = 0.5 * (symmetric + symmetric.T)
    eigenvalues, vectors = jacobi_eigen(symmetric)
    modes = scaling[:, None] * vectors
    return (weights, derivative, stiffness, eigenvalues, modes)


def cosine_modes(count):
    row_pos = np.arange(count)[:, None]
    col_pos = np.arange(count)[None, :]
    scaling = np.where(col_pos == 0, math.sqrt(1.0 / count), math.sqrt(2.0 / count))
    basis_cos = scaling * np.cos(math.pi * col_pos * (row_pos + 0.5) / count)
    eigenvalues = 2.0 - 2.0 * np.cos(math.pi * np.arange(count) / count)
    return (basis_cos, eigenvalues)


def build_tables(count_x, count_y, size_z):
    weights, derivative, stiffness, eigen, modes = gll_tables()
    elem_z = size_z // 8
    lanes = -(-elem_z // 128) * 128
    eye = np.eye(8)
    scaled = stiffness / weights[:, None]
    laplace = np.kron(scaled, eye) + np.kron(eye, scaled)
    left = np.concatenate(
        [
            np.kron(derivative, eye),
            np.kron(eye, derivative),
            viscosity * laplace,
            laplace + pressure_shift * np.eye(64),
            np.kron(modes.T, modes.T),
            np.kron(modes, modes),
        ],
        axis=0,
    )
    blocks = np.eye(16)
    right = np.concatenate(
        [
            np.kron(blocks, matrix).T
            for matrix in (derivative, viscosity * scaled, scaled, modes.T, modes)
        ],
        axis=1,
    )
    weight_xy = np.kron(weights, weights)[:, None]
    weight_3 = weight_xy * np.tile(weights, elem_z)[None, :]
    eigen_xy = (eigen[:, None] + eigen[None, :]).reshape(64, 1)
    inverse = 1.0 / (eigen_xy + np.tile(eigen, elem_z)[None, :] + pressure_shift)
    fields = np.stack([weight_3, inverse])
    modes_y, eig_y = cosine_modes(count_y)
    modes_z, eig_z = cosine_modes(elem_z)
    den = coarse_face * (eig_y[:, None] + eig_z[None, :]) + coarse_reach / float(count_y * count_y)
    down = np.zeros((size_z, lanes))
    down[:, :elem_z] = np.repeat(modes_z, 8, axis=0)
    up = np.zeros((lanes, size_z))
    up[:elem_z] = np.repeat(modes_z, 8, axis=0).T
    green = np.zeros((count_y + 2, count_y, lanes))
    green[1:-1, :, :elem_z] = np.einsum("im,jm,mn->ijn", modes_y, modes_y, 1.0 / den)
    spread = np.repeat(green[1:-1, :, None, :], 8, axis=2)
    spread[:, :, 0] += green[:-2]
    spread[:, :, 7] += green[2:]
    return [
        np.asarray(table, np.float32) for table in (left, right, fields, down, up, spread)
    ]


def dot(a, b):
    return jnp.dot(
        a, b, precision=lax.Precision.HIGHEST, preferred_element_type=jnp.float32
    )


def kernel(
    count_x, count_y, size_b, size_z,
    basis_hbm, base_hbm, left, right, fields, down, up, spread_hbm,
    out, hess,
    basis, base, slopes, spread, field, star, phi, source, state,
    xs3, ys3, cs3, xr3, yr3, cr3,
    xs1, ys1, cs1, xr1, yr1, cr1,
    coarse_s, coarse_r, red_s, red_r,
    load_sem, send3, recv3, send1, recv1, csend, crecv, rsend, rrecv,
):
    gx = lax.axis_index("gx")
    gy = lax.axis_index("gy")
    total = count_x * count_y
    me = gx * count_y + gy
    tiles = size_z // 128

    loads = [
        pltpu.make_async_copy(basis_hbm.at[size_b - 1], basis.at[size_b - 1], load_sem.at[0]),
        pltpu.make_async_copy(base_hbm, base, load_sem.at[1]),
        pltpu.make_async_copy(spread_hbm.at[gy], spread, load_sem.at[2]),
        pltpu.make_async_copy(
            basis_hbm.at[pl.ds(0, size_b - 1)], basis.at[pl.ds(0, size_b - 1)], load_sem.at[3]
        ),
    ]
    for load in loads:
        load.start()
    for buffer in (xr3, yr3, cr3, xr1, yr1, cr1, coarse_r):
        buffer[...] = jnp.zeros_like(buffer)

    barrier = pltpu.get_barrier_semaphore()

    def greet(step, carry):
        other = lax.rem(me + step, total)
        pl.semaphore_signal(
            barrier, inc=1, device_id=(other // count_y, lax.rem(other, count_y)),
            device_id_type=MESH,
        )
        return carry

    lax.fori_loop(1, total, greet, 0)

    def there(dx, dy):
        tests = []
        if dx:
            tests.append((gx > 0) if dx < 0 else (gx < count_x - 1))
        if dy:
            tests.append((gy > 0) if dy < 0 else (gy < count_y - 1))
        return tests[0] if len(tests) == 1 else tests[0] & tests[1]

    row = lax.broadcasted_iota(jnp.int32, (64, size_z), 0)
    lane = lax.broadcasted_iota(jnp.int32, (64, size_z), 1)
    upper_z = (lane % 8 == 7) & (lane < size_z - 1)
    lower_z = (lane % 8 == 0) & (lane > 0)

    def halves(test):
        return jnp.where(test, 0.5, 1.0)

    rmult = (
        halves(((row // 8 == 0) & (gx > 0)) | ((row // 8 == 7) & (gx < count_x - 1)))
        * halves(((row % 8 == 0) & (gy > 0)) | ((row % 8 == 7) & (gy < count_y - 1)))
        * halves(upper_z | lower_z)
    )
    weight_3 = fields.at[0]

    def along_z(f):
        after = pltpu.roll(f, size_z - 1, 1)
        before = pltpu.roll(f, 1, 1)
        return f + jnp.where(upper_z, after, 0.0) + jnp.where(lower_z, before, 0.0)

    def by_left(start, stop, f):
        return dot(left[start:stop, :], f)

    def by_right(start, stop, f):
        stacked = jnp.concatenate([f[:, 128 * t : 128 * t + 128] for t in range(tiles)], axis=0)
        product = dot(stacked, right[:, 128 * start : 128 * stop])
        return [
            jnp.concatenate(
                [product[64 * t : 64 * t + 64, 128 * m : 128 * m + 128] for t in range(tiles)],
                axis=1,
            )
            for m in range(stop - start)
        ]

    def buffers(wide):
        if wide:
            return (xs3, ys3, cs3, xr3, yr3, cr3, send3, recv3)
        return (xs1, ys1, cs1, xr1, yr1, cr1, send1, recv1)

    def each_copy(round_idx, wide, verb):
        xs, ys, cs, xr, yr, cr, ss, rs = buffers(wide)
        for pos, (dx, dy) in enumerate(DIRS):
            ox, oy = (dx + 1) // 2, (dy + 1) // 2
            if dy == 0:
                src, dst, got = xs.at[round_idx, ox], xr.at[round_idx, 1 - ox], xr.at[round_idx, ox]
            elif dx == 0:
                src, dst, got = ys.at[round_idx, oy], yr.at[round_idx, 1 - oy], yr.at[round_idx, oy]
            else:
                src = cs.at[round_idx, 2 * ox + oy]
                dst = cr.at[round_idx, 2 * (1 - ox) + 1 - oy]
                got = cr.at[round_idx, 2 * ox + oy]

            @pl.when(there(dx, dy))
            def _():
                if verb == "start":
                    pltpu.make_async_remote_copy(
                        src_ref=src, dst_ref=dst,
                        send_sem=ss.at[round_idx, pos], recv_sem=rs.at[round_idx, 7 - pos],
                        device_id=(gx + dx, gy + dy), device_id_type=MESH,
                    ).start()
                elif verb == "recv":
                    pltpu.make_async_copy(got, got, rs.at[round_idx, pos]).wait()
                else:
                    pltpu.make_async_copy(src, src, ss.at[round_idx, pos]).wait()

    def cut(value):
        return [value[:, 128 * t : 128 * t + 128] for t in range(tiles)]

    def send(values, round_idx, wide):
        xs, ys, cs = buffers(wide)[:3]
        for c, value in enumerate(values):
            value = along_z(value)
            for t, part in enumerate(cut(value)):
                field[c, t] = part
            xs[round_idx, 0, c] = value[0:8]
            xs[round_idx, 1, c] = value[56:64]
            for o in range(2):
                face = jnp.concatenate(
                    [field[c, t, pl.ds(7 * o, 8, stride=8), :] for t in range(tiles)], axis=1
                )
                ys[round_idx, o, c] = face
                cs[round_idx, o, c] = face[0:1]
                cs[round_idx, 2 + o, c] = face[7:8]
        each_copy(round_idx, wide, "start")

    def receive(count, round_idx, wide):
        xr, yr, cr = buffers(wide)[3:6]
        each_copy(round_idx, wide, "recv")
        results = []
        for c in range(count):
            for t in range(tiles):
                lanes = slice(128 * t, 128 * t + 128)
                field[c, t, 0:8, :] += xr[round_idx, 0, c, :, lanes]
                field[c, t, 56:64, :] += xr[round_idx, 1, c, :, lanes]
                for o in range(2):
                    rows = pl.ds(7 * o, 8, stride=8)
                    field[c, t, rows, :] += yr[round_idx, o, c, :, lanes]
                    field[c, t, 7 * o : 7 * o + 1, :] += cr[round_idx, o, c, :, lanes]
                    field[c, t, 56 + 7 * o : 57 + 7 * o, :] += cr[round_idx, 2 + o, c, :, lanes]
            results.append(jnp.concatenate([field[c, t] for t in range(tiles)], axis=1))
        return results

    loads[0].wait()
    first = [basis[size_b - 1, c] for c in range(3)]
    pl.semaphore_wait(barrier, total - 1)
    send(first, 0, True)
    loads[1].wait()
    for c in range(3):
        value = base[c]
        both = by_left(0, 128, value)
        slopes[0, c] = both[:64]
        slopes[1, c] = both[64:]
        slopes[2, c] = by_right(0, 1, value)[0]
    for c, value in enumerate(receive(3, 0, True)):
        state[c] = value * rmult

    sums = []
    for c in range(3):
        value = state[c]
        products = by_left(0, 192, value)
        along, diffuse = by_right(0, 2, value)
        change = products[128:] + diffuse
        for j, slope in enumerate((products[:64], products[64:128], along)):
            change = change + base[j] * slope + state[j] * slopes[j, c]
        sums.append(change)
    send(sums, 1, True)
    for c, value in enumerate(receive(3, 1, True)):
        star[c] = state[c] - time_step * (value * rmult)

    divergence = (
        by_left(0, 64, star[0]) + by_left(64, 128, star[1]) + by_right(0, 1, star[2])[0]
    )
    source[...] = divergence
    loads[2].wait()

    def coarse_copies(sweep):
        for pos, dx in enumerate((-1, 0, 1)):
            def to(step, carry, dx=dx, pos=pos):
                copy = pltpu.make_async_remote_copy(
                    src_ref=coarse_s.at[sweep],
                    dst_ref=coarse_r.at[sweep, 2 - pos, gy],
                    send_sem=csend.at[sweep, pos],
                    recv_sem=crecv.at[sweep, 2 - pos],
                    device_id=(gx + dx, lax.rem(gy + step, count_y)),
                    device_id_type=MESH,
                )
                copy.start()
                return carry

            if dx == 0:
                lax.fori_loop(1, count_y, to, 0)
            else:
                @pl.when(there(dx, 0))
                def _():
                    lax.fori_loop(0, count_y, to, 0)

    def coarse_wait(sweep, sems):
        for pos, dx in enumerate((-1, 0, 1)):
            part = coarse_r.at[sweep, pos]
            if dx == 0:
                part = coarse_r.at[sweep, pos, pl.ds(0, count_y - 1)]
            if dx == 0:
                pltpu.make_async_copy(part, part, sems.at[sweep, pos]).wait()
            else:

                @pl.when(there(dx, 0))
                def _():
                    pltpu.make_async_copy(part, part, sems.at[sweep, pos]).wait()

    for sweep in range(SWEEPS):
        if sweep == 0:
            whole = source[...]
        else:
            pressure = phi[...]
            whole = source[...] + by_left(192, 256, pressure) + by_right(2, 3, pressure)[0]
        send([-weight_3[...] * whole], 2 * sweep, False)
        resid = receive(1, 2 * sweep, False)[0]
        shares = jnp.sum(resid * rmult, axis=0, keepdims=True)
        shares = dot(jnp.broadcast_to(shares, (8, size_z)), down[...])[0:1]
        coarse_s[sweep] = shares
        coarse_copies(sweep)
        coarse_r[sweep, 1, gy] = shares
        local = by_left(256, 320, resid)
        local = by_right(3, 4, local)[0] * fields[1]
        local = by_left(320, 384, local)
        local = by_right(4, 5, local)[0]
        send([local], 2 * sweep + 1, False)
        coarse_wait(sweep, crecv)
        parts = []
        for pos in range(3):
            part = spread[0] * coarse_r[sweep, pos, 0]
            for j in range(1, count_y):
                part = part + spread[j] * coarse_r[sweep, pos, j]
            parts.append(part)
        levels = dot(jnp.concatenate(parts, axis=0), up[...])
        lower, own, upper = levels[0:8], levels[8:16], levels[16:24]
        flat = jnp.concatenate([own + lower] + [own] * 6 + [own + upper], axis=0)
        step_sum = along_z(flat) + receive(1, 2 * sweep + 1, False)[0]
        update = relaxation * step_sum * rmult
        phi[...] = update if sweep == 0 else phi[...] + update

    pressure = phi[...]
    both = by_left(0, 128, pressure)
    send([both[:64], both[64:], by_right(0, 1, pressure)[0]], 2, True)
    for c, value in enumerate(receive(3, 2, True)):
        star[c] = star[c] - value * rmult
    loads[3].wait()
    mass = weight_3[...] * rmult * (1.0 / (8.0 * total * (size_z // 8)))
    phi[...] = mass

    def fold(value):
        return functools.reduce(
            lambda a, b: a + b, [value[:, 128 * t : 128 * t + 128] for t in range(tiles)]
        )

    def products_of(step, sums):
        c, x = step // 8, lax.rem(step, 8)
        rows = pl.ds(pl.multiple_of(8 * x, 8), 8)
        weighted = star[c, rows, :] * phi[rows, :]
        return tuple(
            total_k + fold(basis[k, c, rows, :] * weighted) for k, total_k in enumerate(sums)
        )

    zero = jnp.zeros((8, 128), jnp.float32)
    sums = lax.fori_loop(0, 24, products_of, (zero,) * size_b)
    lane_1 = lax.broadcasted_iota(jnp.int32, (1, 128), 1)

    def all_sum(which, value):
        red_s[which] = value

        def to(step, carry):
            other = lax.rem(me + step, total)
            pltpu.make_async_remote_copy(
                src_ref=red_s.at[which], dst_ref=red_r.at[which, me],
                send_sem=rsend.at[which], recv_sem=rrecv.at[which],
                device_id=(other // count_y, lax.rem(other, count_y)), device_id_type=MESH,
            ).start()
            return carry

        lax.fori_loop(1, total, to, 0)
        red_r[which, me] = value
        part = red_r.at[which, pl.ds(0, total - 1)]
        pltpu.make_async_copy(part, part, rrecv.at[which]).wait()
        return functools.reduce(lambda a, b: a + b, [red_r[which, j] for j in range(total)])

    own = jnp.zeros((1, 128), jnp.float32)
    for k in range(size_b):
        value = jnp.sum(jnp.sum(sums[k], axis=0, keepdims=True), axis=1, keepdims=True)
        own = jnp.where(lane_1 == k, value, own)
    hcol = all_sum(0, own)
    spreads = [
        jnp.broadcast_to(
            jnp.sum(jnp.where(lane_1 == k, hcol, 0.0), axis=1, keepdims=True), (8, 128)
        )
        for k in range(size_b)
    ]

    def remainder_of(step, squares):
        c, x = step // 8, lax.rem(step, 8)
        rows = pl.ds(pl.multiple_of(8 * x, 8), 8)
        for t in range(tiles):
            lanes = slice(128 * t, 128 * t + 128)
            value = star[c, rows, lanes]
            for k in range(size_b):
                value = value - spreads[k] * basis[k, c, rows, lanes]
            star[c, rows, lanes] = value
            squares = squares + value * value * phi[rows, lanes]
        return squares

    squares = lax.fori_loop(0, 24, remainder_of, zero)
    squared = jnp.sum(jnp.sum(squares, axis=0, keepdims=True), axis=1, keepdims=True)
    squared = all_sum(1, jnp.broadcast_to(squared, (1, 128)))
    beta = jnp.sqrt(squared + norm_eps)
    hess[...] = jnp.where(lane_1 == size_b, beta, hcol)
    scale = 1.0 / beta[:, 0:1]
    for c in range(3):
        out[c] = star[c] * scale

    for round_idx in range(3):
        each_copy(round_idx, True, "sent")
    for round_idx in range(2 * SWEEPS):
        each_copy(round_idx, False, "sent")
    for sweep in range(SWEEPS):
        coarse_wait(sweep, csend)
    for which in range(2):
        part = red_r.at[which, pl.ds(0, total - 1)]
        pltpu.make_async_copy(part, part, rsend.at[which]).wait()


def per_device(basis, base_flow):
    size_b = basis.shape[0]
    components, size_x, size_y, size_z = base_flow.shape
    count_x = lax.axis_size("gx")
    count_y = lax.axis_size("gy")
    tables = build_tables(count_x, count_y, size_z)
    lanes = tables[3].shape[1]
    vmem = functools.partial(pltpu.VMEM, dtype=jnp.float32)
    dma = pltpu.SemaphoreType.DMA
    exchange = []
    for rounds, comps in ((3, 3), (2 * SWEEPS, 1)):
        shapes = [
            (rounds, 2, comps, 8, size_z),
            (rounds, 2, comps, 8, size_z),
            (rounds, 4, comps, 1, size_z),
        ]
        exchange += [vmem(shape) for shape in shapes * 2]
    spec_v = pl.BlockSpec(memory_space=pltpu.VMEM)
    spec_any = pl.BlockSpec(memory_space=pl.ANY)
    out, hess = pl.pallas_call(
        functools.partial(kernel, count_x, count_y, size_b, size_z),
        out_shape=(
            jax.ShapeDtypeStruct((3, 64, size_z), jnp.float32),
            jax.ShapeDtypeStruct((1, 128), jnp.float32),
        ),
        in_specs=[spec_any, spec_any] + [spec_v] * 5 + [spec_any],
        out_specs=(spec_v, spec_v),
        scratch_shapes=[
            vmem((size_b, 3, 64, size_z)),
            vmem((3, 64, size_z)),
            vmem((3, 3, 64, size_z)),
            vmem((count_y, 8, lanes)),
            vmem((3, size_z // 128, 64, 128)),
            vmem((3, 64, size_z)),
            vmem((64, size_z)),
            vmem((64, size_z)),
            vmem((3, 64, size_z)),
        ]
        + exchange
        + [
            vmem((SWEEPS, 1, lanes)),
            vmem((SWEEPS, 3, count_y, 1, lanes)),
            vmem((2, 1, 128)),
            vmem((2, count_x * count_y, 1, 128)),
            dma((4,)),
            dma((3, 8)),
            dma((3, 8)),
            dma((2 * SWEEPS, 8)),
            dma((2 * SWEEPS, 8)),
            dma((SWEEPS, 3)),
            dma((SWEEPS, 3)),
            dma((2,)),
            dma((2,)),
        ],
        compiler_params=pltpu.CompilerParams(
            collective_id=0, has_side_effects=True, vmem_limit_bytes=48 * 1024 * 1024
        ),
    )(
        basis.reshape(size_b, 3, 64, size_z),
        base_flow.reshape(3, 64, size_z),
        *[jnp.asarray(table) for table in tables],
    )
    return (out.reshape(base_flow.shape), hess[0, : size_b + 1])


def solution(mesh):
    return jax.shard_map(
        per_device,
        mesh=mesh,
        in_specs=(P(None, None, "gx", "gy", None), P(None, "gx", "gy", None)),
        out_specs=(P(None, "gx", "gy", None), P()),
        check_vma=False,
    )
```

profile of v0, /device:TPU:0, one launch (start us, length us, event | category | flops | bytes accessed | tf_op | source)
XLA Modules:
  0.0 78.8 jit_solution(10891497405545963905)
XLA Ops:
  0.6 0.0 copy-start
  0.6 1.0 %copy-done = f32[3,8,8,512]{3,2,1,0:T(8,128)S(1)} copy-done((f32[3,8,8,512]{3,2,1,0:T(8,128)S(1)}, f32[3,8,8,512]{3,2,1,0:T(8,128)}, u32[]{:S(2)}) %copy-start) | copy-done | bytes 393240
  1.6 0.0 copy-start.1
  1.6 1.0 %copy-done.1 = f32[128,640]{1,0:T(8,128)S(1)} copy-done((f32[128,640]{1,0:T(8,128)S(1)}, f32[128,640]{1,0:T(8,128)}, u32[]{:S(2)}) %copy-start.1) | copy-done | bytes 327704
  2.6 0.0 copy-start.2
  2.6 0.9 %copy-done.2 = f32[8,8,8,128]{3,2,1,0:T(8,128)S(1)} copy-done((f32[8,8,8,128]{3,2,1,0:T(8,128)S(1)}, f32[8,8,8,128]{3,2,1,0:T(8,128)}, u32[]{:S(2)}) %copy-start.2) | copy-done | bytes 262168
  3.5 0.0 copy-start.3
  3.6 0.9 %copy-done.3 = f32[128,512]{1,0:T(8,128)S(1)} copy-done((f32[128,512]{1,0:T(8,128)S(1)}, f32[128,512]{1,0:T(8,128)}, u32[]{:S(2)}) %copy-start.3) | copy-done | bytes 262168
  4.5 0.0 copy-start.4
  4.5 0.9 %copy-done.4 = f32[512,128]{1,0:T(8,128)S(1)} copy-done((f32[512,128]{1,0:T(8,128)S(1)}, f32[512,128]{1,0:T(8,128)}, u32[]{:S(2)}) %copy-start.4) | copy-done | bytes 262168
  5.5 0.0 copy-start.5
  5.5 0.9 %copy-done.5 = f32[2,64,512]{2,1,0:T(8,128)S(1)} copy-done((f32[2,64,512]{2,1,0:T(8,128)S(1)}, f32[2,64,512]{2,1,0:T(8,128)}, u32[]{:S(2)}) %copy-start.5) | copy-done | bytes 262168
  6.4 0.0 copy-start.6
  6.4 0.9 %copy-done.6 = f32[384,64]{1,0:T(8,128)S(1)} copy-done((f32[384,64]{1,0:T(8,128)S(1)}, f32[384,64]{1,0:T(8,128)}, u32[]{:S(2)}) %copy-start.6) | copy-done | bytes 98328
  7.3 70.2 %shard_map.95 = (f32[3,64,512]{2,1,0:T(8,128)S(1)}, f32[1,128]{1,0:T(1,128)S(1)}) custom-call(f32[20,3,64,512]{3,2,1,0:T(8,128)} %bitcast.7, f32[3,64,512]{2,1,0:T(8,128)S(1)} %bitcast.5, f32[384,64]{1,0:T(8,128)S(1)} %copy-done.6, f32[128,640]{1,0:T(8,128)S(1)} %copy-done.1, f32[2,64,512]{2,1,0:T(8,128)S(1)} %copy-done.5, f32[512,128]{1,0:T(8,128)S(1)} %copy-done.4, ...), custom_call_target="tpu_custom_call" | custom-call | tf_op jit(solution)/shard_map/pallas_call | solution.py:504
  77.5 0.5 slice_bitcast_fusion
  78.0 0.7 copy.11
Async XLA Ops:
  0.6 1.0 %copy-start = (f32[3,8,8,512]{3,2,1,0:T(8,128)S(1)}, f32[3,8,8,512]{3,2,1,0:T(8,128)}, u32[]{:S(2)}) copy-start(f32[3,8,8,512]{3,2,1,0:T(8,128)} %param.9) | copy-start | bytes 1179652
  1.6 1.0 %copy-start.1 = (f32[128,640]{1,0:T(8,128)S(1)}, f32[128,640]{1,0:T(8,128)}, u32[]{:S(2)}) copy-start(f32[128,640]{1,0:T(8,128)} %constant.13.clone.right) | copy-start | bytes 983044
  2.6 0.9 %copy-start.2 = (f32[8,8,8,128]{3,2,1,0:T(8,128)S(1)}, f32[8,8,8,128]{3,2,1,0:T(8,128)}, u32[]{:S(2)}) copy-start(f32[8,8,8,128]{3,2,1,0:T(8,128)} %constant.17.clone.spread_hbm) | copy-start | bytes 786436
  3.5 0.9 %copy-start.3 = (f32[128,512]{1,0:T(8,128)S(1)}, f32[128,512]{1,0:T(8,128)}, u32[]{:S(2)}) copy-start(f32[128,512]{1,0:T(8,128)} %constant.16.clone.up) | copy-start | bytes 786436
  4.5 0.9 %copy-start.4 = (f32[512,128]{1,0:T(8,128)S(1)}, f32[512,128]{1,0:T(8,128)}, u32[]{:S(2)}) copy-start(f32[512,128]{1,0:T(8,128)} %constant.15.clone.down) | copy-start | bytes 786436
  5.5 0.9 %copy-start.5 = (f32[2,64,512]{2,1,0:T(8,128)S(1)}, f32[2,64,512]{2,1,0:T(8,128)}, u32[]{:S(2)}) copy-start(f32[2,64,512]{2,1,0:T(8,128)} %constant.14.clone.fields) | copy-start | bytes 786436
  6.4 0.9 %copy-start.6 = (f32[384,64]{1,0:T(8,128)S(1)}, f32[384,64]{1,0:T(8,128)}, u32[]{:S(2)}) copy-start(f32[384,64]{1,0:T(8,128)} %constant.12.clone.left) | copy-start | bytes 294916
where the time goes:
time: 79.1 us; the launch traced here: 78.8 us
  Pallas kernels  70.2 us (89%)
  local copies, waits for them, and re-layouts  7.94 us (10%)
    pallas_call x1, Pallas kernels, per_device(): pl.pallas_call(functools.partial(kernel, count_x, count_y, size_b, size_z...  70.2 us
    unnamed x15, local copies, waits for them, and re-layouts  7.43 us

commit v1 on v0

--- a/solution.py
+++ b/solution.py
@@ -88,6 +88,11 @@
     basis_cos = scaling * np.cos(math.pi * col_pos * (row_pos + 0.5) / count)
     eigenvalues = 2.0 - 2.0 * np.cos(math.pi * np.arange(count) / count)
     return (basis_cos, eigenvalues)
+
+
+def halved(table):
+    high = table.astype(jnp.bfloat16)
+    return high, (table - high.astype(np.float64)).astype(jnp.bfloat16)
 
 
 def build_tables(count_x, count_y, size_z):
@@ -133,22 +138,33 @@
     spread = np.repeat(green[1:-1, :, None, :], 8, axis=2)
     spread[:, :, 0] += green[:-2]
     spread[:, :, 7] += green[2:]
+    left_hi, left_lo = halved(left)
+    right_hi, right_lo = halved(right)
+    up_hi, up_lo = halved(up)
     return [
-        np.asarray(table, np.float32) for table in (left, right, fields, down, up, spread)
+        np.concatenate([left_hi, left_hi, left_lo], axis=1),
+        np.concatenate([right_hi, right_hi, right_lo], axis=0),
+        np.asarray(fields, np.float32),
+        np.concatenate(halved(down), axis=1),
+        np.concatenate([up_hi, up_hi, up_lo], axis=0),
+        np.asarray(spread, np.float32),
     ]
 
 
+def split(value):
+    high = value.astype(jnp.bfloat16)
+    return high, (value - high.astype(jnp.float32)).astype(jnp.bfloat16)
+
+
 def dot(a, b):
-    return jnp.dot(
-        a, b, precision=lax.Precision.HIGHEST, preferred_element_type=jnp.float32
-    )
+    return jnp.dot(a, b, preferred_element_type=jnp.float32)
 
 
 def kernel(
     count_x, count_y, size_b, size_z,
-    basis_hbm, base_hbm, left, right, fields, down, up, spread_hbm,
+    basis_hbm, base_hbm, left_hbm, right_hbm, fields_hbm, down_hbm, up_hbm, spread_hbm,
     out, hess,
-    basis, base, slopes, spread, field, star, phi, source, state,
+    basis, base, left, right, fields, down, up, slopes, spread, field, star, phi, source, state,
     xs3, ys3, cs3, xr3, yr3, cr3,
     xs1, ys1, cs1, xr1, yr1, cr1,
     coarse_s, coarse_r, red_s, red_r,
@@ -159,6 +175,7 @@
     total = count_x * count_y
     me = gx * count_y + gy
     tiles = size_z // 128
+    width = coarse_s.shape[-1]
 
     loads = [
         pltpu.make_async_copy(basis_hbm.at[size_b - 1], basis.at[size_b - 1], load_sem.at[0]),
@@ -167,9 +184,14 @@
         pltpu.make_async_copy(
             basis_hbm.at[pl.ds(0, size_b - 1)], basis.at[pl.ds(0, size_b - 1)], load_sem.at[3]
         ),
+        pltpu.make_async_copy(left_hbm, left, load_sem.at[4]),
+        pltpu.make_async_copy(right_hbm, right, load_sem.at[5]),
+        pltpu.make_async_copy(fields_hbm, fields, load_sem.at[6]),
+        pltpu.make_async_copy(down_hbm, down, load_sem.at[7]),
+        pltpu.make_async_copy(up_hbm, up, load_sem.at[8]),
     ]
-    for load in loads:
-        load.start()
+    for pos in (0, 1, 4, 5, 2, 6, 7, 8):
+        loads[pos].start()
     for buffer in (xr3, yr3, cr3, xr1, yr1, cr1, coarse_r):
         buffer[...] = jnp.zeros_like(buffer)
 
@@ -214,11 +236,15 @@
         return f + jnp.where(upper_z, after, 0.0) + jnp.where(lower_z, before, 0.0)
 
     def by_left(start, stop, f):
-        return dot(left[start:stop, :], f)
+        high, low = split(f)
+        return dot(left[start:stop, :], jnp.concatenate([high, low, high], axis=0))
 
     def by_right(start, stop, f):
         stacked = jnp.concatenate([f[:, 128 * t : 128 * t + 128] for t in range(tiles)], axis=0)
-        product = dot(stacked, right[:, 128 * start : 128 * stop])
+        high, low = split(stacked)
+        product = dot(
+            jnp.concatenate([high, low, high], axis=1), right[:, 128 * start : 128 * stop]
+        )
         return [
             jnp.concatenate(
                 [product[64 * t : 64 * t + 64, 128 * m : 128 * m + 128] for t in range(tiles)],
@@ -299,7 +325,9 @@
     first = [basis[size_b - 1, c] for c in range(3)]
     pl.semaphore_wait(barrier, total - 1)
     send(first, 0, True)
-    loads[1].wait()
+    loads[3].start()
+    for pos in (1, 4, 5):
+        loads[pos].wait()
     for c in range(3):
         value = base[c]
         both = by_left(0, 128, value)
@@ -326,7 +354,8 @@
         by_left(0, 64, star[0]) + by_left(64, 128, star[1]) + by_right(0, 1, star[2])[0]
     )
     source[...] = divergence
-    loads[2].wait()
+    for pos in (2, 6, 7, 8):
+        loads[pos].wait()
 
     def coarse_copies(sweep):
         for pos, dx in enumerate((-1, 0, 1)):
@@ -370,8 +399,14 @@
             whole = source[...] + by_left(192, 256, pressure) + by_right(2, 3, pressure)[0]
         send([-weight_3[...] * whole], 2 * sweep, False)
         resid = receive(1, 2 * sweep, False)[0]
-        shares = jnp.sum(resid * rmult, axis=0, keepdims=True)
-        shares = dot(jnp.broadcast_to(shares, (8, size_z)), down[...])[0:1]
+        shares = functools.reduce(
+            lambda a, b: a + b, [(resid * rmult)[8 * j : 8 * j + 8] for j in range(8)]
+        )
+        shares = dot(jnp.concatenate(split(shares), axis=0), down[...])
+        shares = jnp.sum(
+            shares[0:8, :width] + shares[8:16, :width] + shares[0:8, width:],
+            axis=0, keepdims=True,
+        )
         coarse_s[sweep] = shares
         coarse_copies(sweep)
         coarse_r[sweep, 1, gy] = shares
@@ -387,7 +422,8 @@
             for j in range(1, count_y):
                 part = part + spread[j] * coarse_r[sweep, pos, j]
             parts.append(part)
-        levels = dot(jnp.concatenate(parts, axis=0), up[...])
+        high, low = split(jnp.concatenate(parts, axis=0))
+        levels = dot(jnp.concatenate([high, low, high], axis=1), up[...])
         lower, own, upper = levels[0:8], levels[8:16], levels[16:24]
         flat = jnp.concatenate([own + lower] + [own] * 6 + [own + upper], axis=0)
         step_sum = along_z(flat) + receive(1, 2 * sweep + 1, False)[0]
@@ -488,7 +524,7 @@
     count_x = lax.axis_size("gx")
     count_y = lax.axis_size("gy")
     tables = build_tables(count_x, count_y, size_z)
-    lanes = tables[3].shape[1]
+    lanes = tables[5].shape[3]
     vmem = functools.partial(pltpu.VMEM, dtype=jnp.float32)
     dma = pltpu.SemaphoreType.DMA
     exchange = []
@@ -507,11 +543,14 @@
             jax.ShapeDtypeStruct((3, 64, size_z), jnp.float32),
             jax.ShapeDtypeStruct((1, 128), jnp.float32),
         ),
-        in_specs=[spec_any, spec_any] + [spec_v] * 5 + [spec_any],
+        in_specs=[spec_any] * 8,
         out_specs=(spec_v, spec_v),
         scratch_shapes=[
             vmem((size_b, 3, 64, size_z)),
             vmem((3, 64, size_z)),
+        ]
+        + [pltpu.VMEM(table.shape, table.dtype) for table in tables[:5]]
+        + [
             vmem((3, 3, 64, size_z)),
             vmem((count_y, 8, lanes)),
             vmem((3, size_z // 128, 64, 128)),
@@ -526,7 +565,7 @@
             vmem((SWEEPS, 3, count_y, 1, lanes)),
             vmem((2, 1, 128)),
             vmem((2, count_x * count_y, 1, 128)),
-            dma((4,)),
+            dma((9,)),
             dma((3, 8)),
             dma((3, 8)),
             dma((2 * SWEEPS, 8)),
@@ -537,7 +576,7 @@
             dma((2,)),
         ],
         compiler_params=pltpu.CompilerParams(
-            collective_id=0, has_side_effects=True, vmem_limit_bytes=48 * 1024 * 1024
+            collective_id=0, has_side_effects=True, vmem_limit_bytes=60 * 1024 * 1024
         ),
     )(
         basis.reshape(size_b, 3, 64, size_z),

time: 79.1 us -> 68.6 us (0.87)
  Pallas kernels: 70.2 us -> 64.9 us
  local copies, waits for them, and re-layouts: 7.94 us -> 2.89 us
    unnamed x15 -> x1, local copies, waits for them, and re-layouts: 7.43 us -> 1.77 us
    pallas_call x1, Pallas kernels: 70.2 us -> 64.9 us  [per_device(): pl.pallas_call(functools.partial(kernel, count_x, count_y, size_b, size_z...]
where the time goes in v1:
time: 68.6 us; the launch traced here: 68.5 us
  Pallas kernels  64.9 us (95%)
  local copies, waits for them, and re-layouts  2.89 us (4%)
    pallas_call x1, Pallas kernels, per_device(): pl.pallas_call(functools.partial(kernel, count_x, count_y, size_b, size_z...  64.9 us
    unnamed x1, local copies, waits for them, and re-layouts  1.77 us

profile of v1, /device:TPU:0, one launch (start us, length us, event | category | flops | bytes accessed | tf_op | source)
XLA Modules:
  0.0 68.5 jit_solution(13334669747408930670)
XLA Ops:
  0.6 64.9 %shard_map.95 = (f32[3,64,512]{2,1,0:T(8,128)}, f32[1,128]{1,0:T(1,128)}) custom-call(f32[20,3,64,512]{3,2,1,0:T(8,128)} %bitcast.5, f32[3,64,512]{2,1,0:T(8,128)} %bitcast.6, bf16[384,192]{1,0:T(8,128)(2,1)} %constant.12.clone.left_hbm, bf16[384,640]{1,0:T(8,128)(2,1)} %constant.13.clone.right_hbm, f32[2,64,512]{2,1,0:T(8,128)} %constant.14.clone.fields_hbm, ...), custom_call_target="tpu_custom_call" | custom-call | tf_op jit(solution)/shard_map/pallas_call | solution.py:540
  65.6 1.1 %slice_bitcast_fusion = f32[21]{0:T(128)} fusion(f32[1,128]{1,0:T(1,128)} %get-tuple-element.5), kind=kLoop, calls=%fused_computation | loop fusion | bytes 168 | tf_op jit(solution)/shard_map/squeeze | solution.py:586
  66.7 1.8 %copy.11 = f32[3,8,8,512]{3,2,1,0:T(8,128)} copy(f32[3,8,8,512]{3,2,1,0:T(8,128)} %bitcast.7) | data formatting | bytes 786432

commit v2 on v1

--- a/solution.py
+++ b/solution.py
@@ -165,10 +165,9 @@
     basis_hbm, base_hbm, left_hbm, right_hbm, fields_hbm, down_hbm, up_hbm, spread_hbm,
     out, hess,
     basis, base, left, right, fields, down, up, slopes, spread, field, star, phi, source, state,
-    xs3, ys3, cs3, xr3, yr3, cr3,
-    xs1, ys1, cs1, xr1, yr1, cr1,
+    xs, ys, cs, xr, yr, cr,
     coarse_s, coarse_r, red_s, red_r,
-    load_sem, send3, recv3, send1, recv1, csend, crecv, rsend, rrecv,
+    load_sem, fsend, frecv, csend, crecv, rsend, rrecv,
 ):
     gx = lax.axis_index("gx")
     gy = lax.axis_index("gy")
@@ -192,9 +191,6 @@
     ]
     for pos in (0, 1, 4, 5, 2, 6, 7, 8):
         loads[pos].start()
-    for buffer in (xr3, yr3, cr3, xr1, yr1, cr1, coarse_r):
-        buffer[...] = jnp.zeros_like(buffer)
-
     barrier = pltpu.get_barrier_semaphore()
 
     def greet(step, carry):
@@ -215,6 +211,22 @@
             tests.append((gy > 0) if dy < 0 else (gy < count_y - 1))
         return tests[0] if len(tests) == 1 else tests[0] & tests[1]
 
+    def clear(ref):
+        ref[...] = jnp.zeros(ref.shape, ref.dtype)
+
+    for dx, dy in DIRS:
+        ox, oy = (dx + 1) // 2, (dy + 1) // 2
+
+        @pl.when(jnp.logical_not(there(dx, dy)))
+        def _():
+            if dy == 0:
+                clear(xr.at[:, ox])
+                clear(coarse_r.at[:, 2 * ox])
+            elif dx == 0:
+                clear(yr.at[:, oy])
+            else:
+                clear(cr.at[:, 2 * ox + oy])
+
     row = lax.broadcasted_iota(jnp.int32, (64, size_z), 0)
     lane = lax.broadcasted_iota(jnp.int32, (64, size_z), 1)
     upper_z = (lane % 8 == 7) & (lane < size_z - 1)
@@ -253,13 +265,7 @@
             for m in range(stop - start)
         ]
 
-    def buffers(wide):
-        if wide:
-            return (xs3, ys3, cs3, xr3, yr3, cr3, send3, recv3)
-        return (xs1, ys1, cs1, xr1, yr1, cr1, send1, recv1)
-
-    def each_copy(round_idx, wide, verb):
-        xs, ys, cs, xr, yr, cr, ss, rs = buffers(wide)
+    def each_copy(round_idx, verb):
         for pos, (dx, dy) in enumerate(DIRS):
             ox, oy = (dx + 1) // 2, (dy + 1) // 2
             if dy == 0:
@@ -276,55 +282,49 @@
                 if verb == "start":
                     pltpu.make_async_remote_copy(
                         src_ref=src, dst_ref=dst,
-                        send_sem=ss.at[round_idx, pos], recv_sem=rs.at[round_idx, 7 - pos],
+                        send_sem=fsend.at[round_idx, pos], recv_sem=frecv.at[round_idx, 7 - pos],
                         device_id=(gx + dx, gy + dy), device_id_type=MESH,
                     ).start()
                 elif verb == "recv":
-                    pltpu.make_async_copy(got, got, rs.at[round_idx, pos]).wait()
+                    pltpu.make_async_copy(got, got, frecv.at[round_idx, pos]).wait()
                 else:
-                    pltpu.make_async_copy(src, src, ss.at[round_idx, pos]).wait()
+                    pltpu.make_async_copy(src, src, fsend.at[round_idx, pos]).wait()
 
     def cut(value):
         return [value[:, 128 * t : 128 * t + 128] for t in range(tiles)]
 
-    def send(values, round_idx, wide):
-        xs, ys, cs = buffers(wide)[:3]
-        for c, value in enumerate(values):
-            value = along_z(value)
-            for t, part in enumerate(cut(value)):
-                field[c, t] = part
-            xs[round_idx, 0, c] = value[0:8]
-            xs[round_idx, 1, c] = value[56:64]
+    def send(value, round_idx, c=0):
+        value = along_z(value)
+        for t, part in enumerate(cut(value)):
+            field[c, t] = part
+        xs[round_idx, 0] = value[0:8]
+        xs[round_idx, 1] = value[56:64]
+        for o in range(2):
+            face = jnp.concatenate(
+                [field[c, t, pl.ds(7 * o, 8, stride=8), :] for t in range(tiles)], axis=1
+            )
+            ys[round_idx, o] = face
+            cs[round_idx, o] = face[0:1]
+            cs[round_idx, 2 + o] = face[7:8]
+        each_copy(round_idx, "start")
+
+    def receive(round_idx, c=0):
+        each_copy(round_idx, "recv")
+        for t in range(tiles):
+            lanes = slice(128 * t, 128 * t + 128)
+            field[c, t, 0:8, :] += xr[round_idx, 0, :, lanes]
+            field[c, t, 56:64, :] += xr[round_idx, 1, :, lanes]
             for o in range(2):
-                face = jnp.concatenate(
-                    [field[c, t, pl.ds(7 * o, 8, stride=8), :] for t in range(tiles)], axis=1
-                )
-                ys[round_idx, o, c] = face
-                cs[round_idx, o, c] = face[0:1]
-                cs[round_idx, 2 + o, c] = face[7:8]
-        each_copy(round_idx, wide, "start")
-
-    def receive(count, round_idx, wide):
-        xr, yr, cr = buffers(wide)[3:6]
-        each_copy(round_idx, wide, "recv")
-        results = []
-        for c in range(count):
-            for t in range(tiles):
-                lanes = slice(128 * t, 128 * t + 128)
-                field[c, t, 0:8, :] += xr[round_idx, 0, c, :, lanes]
-                field[c, t, 56:64, :] += xr[round_idx, 1, c, :, lanes]
-                for o in range(2):
-                    rows = pl.ds(7 * o, 8, stride=8)
-                    field[c, t, rows, :] += yr[round_idx, o, c, :, lanes]
-                    field[c, t, 7 * o : 7 * o + 1, :] += cr[round_idx, o, c, :, lanes]
-                    field[c, t, 56 + 7 * o : 57 + 7 * o, :] += cr[round_idx, 2 + o, c, :, lanes]
-            results.append(jnp.concatenate([field[c, t] for t in range(tiles)], axis=1))
-        return results
+                rows = pl.ds(7 * o, 8, stride=8)
+                field[c, t, rows, :] += yr[round_idx, o, :, lanes]
+                field[c, t, 7 * o : 7 * o + 1, :] += cr[round_idx, o, :, lanes]
+                field[c, t, 56 + 7 * o : 57 + 7 * o, :] += cr[round_idx, 2 + o, :, lanes]
+        return jnp.concatenate([field[c, t] for t in range(tiles)], axis=1)
 
     loads[0].wait()
-    first = [basis[size_b - 1, c] for c in range(3)]
     pl.semaphore_wait(barrier, total - 1)
-    send(first, 0, True)
+    for c in range(3):
+        send(basis[size_b - 1, c], c, c)
     loads[3].start()
     for pos in (1, 4, 5):
         loads[pos].wait()
@@ -334,10 +334,9 @@
         slopes[0, c] = both[:64]
         slopes[1, c] = both[64:]
         slopes[2, c] = by_right(0, 1, value)[0]
-    for c, value in enumerate(receive(3, 0, True)):
-        state[c] = value * rmult
-
-    sums = []
+    for c in range(3):
+        state[c] = receive(c, c) * rmult
+
     for c in range(3):
         value = state[c]
         products = by_left(0, 192, value)
@@ -345,10 +344,9 @@
         change = products[128:] + diffuse
         for j, slope in enumerate((products[:64], products[64:128], along)):
             change = change + base[j] * slope + state[j] * slopes[j, c]
-        sums.append(change)
-    send(sums, 1, True)
-    for c, value in enumerate(receive(3, 1, True)):
-        star[c] = state[c] - time_step * (value * rmult)
+        send(change, 3 + c, c)
+    for c in range(3):
+        star[c] = state[c] - time_step * (receive(3 + c, c) * rmult)
 
     divergence = (
         by_left(0, 64, star[0]) + by_left(64, 128, star[1]) + by_right(0, 1, star[2])[0]
@@ -397,8 +395,8 @@
         else:
             pressure = phi[...]
             whole = source[...] + by_left(192, 256, pressure) + by_right(2, 3, pressure)[0]
-        send([-weight_3[...] * whole], 2 * sweep, False)
-        resid = receive(1, 2 * sweep, False)[0]
+        send(-weight_3[...] * whole, 9 + 2 * sweep)
+        resid = receive(9 + 2 * sweep)
         shares = functools.reduce(
             lambda a, b: a + b, [(resid * rmult)[8 * j : 8 * j + 8] for j in range(8)]
         )
@@ -414,7 +412,7 @@
         local = by_right(3, 4, local)[0] * fields[1]
         local = by_left(320, 384, local)
         local = by_right(4, 5, local)[0]
-        send([local], 2 * sweep + 1, False)
+        send(local, 10 + 2 * sweep)
         coarse_wait(sweep, crecv)
         parts = []
         for pos in range(3):
@@ -426,15 +424,17 @@
         levels = dot(jnp.concatenate([high, low, high], axis=1), up[...])
         lower, own, upper = levels[0:8], levels[8:16], levels[16:24]
         flat = jnp.concatenate([own + lower] + [own] * 6 + [own + upper], axis=0)
-        step_sum = along_z(flat) + receive(1, 2 * sweep + 1, False)[0]
+        step_sum = along_z(flat) + receive(10 + 2 * sweep)
         update = relaxation * step_sum * rmult
         phi[...] = update if sweep == 0 else phi[...] + update
 
     pressure = phi[...]
     both = by_left(0, 128, pressure)
-    send([both[:64], both[64:], by_right(0, 1, pressure)[0]], 2, True)
-    for c, value in enumerate(receive(3, 2, True)):
-        star[c] = star[c] - value * rmult
+    send(both[:64], 6, 0)
+    send(both[64:], 7, 1)
+    send(by_right(0, 1, pressure)[0], 8, 2)
+    for c in range(3):
+        star[c] = star[c] - receive(6 + c, c) * rmult
     loads[3].wait()
     mass = weight_3[...] * rmult * (1.0 / (8.0 * total * (size_z // 8)))
     phi[...] = mass
@@ -507,10 +507,8 @@
     for c in range(3):
         out[c] = star[c] * scale
 
-    for round_idx in range(3):
-        each_copy(round_idx, True, "sent")
-    for round_idx in range(2 * SWEEPS):
-        each_copy(round_idx, False, "sent")
+    for round_idx in range(9 + 2 * SWEEPS):
+        each_copy(round_idx, "sent")
     for sweep in range(SWEEPS):
         coarse_wait(sweep, csend)
     for which in range(2):
@@ -527,14 +525,9 @@
     lanes = tables[5].shape[3]
     vmem = functools.partial(pltpu.VMEM, dtype=jnp.float32)
     dma = pltpu.SemaphoreType.DMA
-    exchange = []
-    for rounds, comps in ((3, 3), (2 * SWEEPS, 1)):
-        shapes = [
-            (rounds, 2, comps, 8, size_z),
-            (rounds, 2, comps, 8, size_z),
-            (rounds, 4, comps, 1, size_z),
-        ]
-        exchange += [vmem(shape) for shape in shapes * 2]
+    rounds = 9 + 2 * SWEEPS
+    shapes = [(rounds, 2, 8, size_z), (rounds, 2, 8, size_z), (rounds, 4, 1, size_z)]
+    exchange = [vmem(shape) for shape in shapes * 2]
     spec_v = pl.BlockSpec(memory_space=pltpu.VMEM)
     spec_any = pl.BlockSpec(memory_space=pl.ANY)
     out, hess = pl.pallas_call(
@@ -566,10 +559,8 @@
             vmem((2, 1, 128)),
             vmem((2, count_x * count_y, 1, 128)),
             dma((9,)),
-            dma((3, 8)),
-            dma((3, 8)),
-            dma((2 * SWEEPS, 8)),
-            dma((2 * SWEEPS, 8)),
+            dma((rounds, 8)),
+            dma((rounds, 8)),
             dma((SWEEPS, 3)),
             dma((SWEEPS, 3)),
             dma((2,)),

time: 68.6 us -> 69.5 us (1.013)
  Pallas kernels: 64.9 us -> 65.8 us
    pallas_call x1, Pallas kernels: 64.9 us -> 65.8 us  [per_device(): pl.pallas_call(functools.partial(kernel, count_x, count_y, size_b, size_z...]
where the time goes in v2:
time: 69.5 us; the launch traced here: 69.3 us
  Pallas kernels  65.8 us (95%)
  local copies, waits for them, and re-layouts  2.89 us (4%)
    pallas_call x1, Pallas kernels, per_device(): pl.pallas_call(functools.partial(kernel, count_x, count_y, size_b, size_z...  65.8 us
    unnamed x1, local copies, waits for them, and re-layouts  1.77 us

profile of v2, /device:TPU:0, one launch (start us, length us, event | category | flops | bytes accessed | tf_op | source)
XLA Modules:
  0.0 69.3 jit_solution(8770619013573148917)
XLA Ops:
  0.6 65.8 %shard_map.95 = (f32[3,64,512]{2,1,0:T(8,128)}, f32[1,128]{1,0:T(1,128)}) custom-call(f32[20,3,64,512]{3,2,1,0:T(8,128)} %bitcast.5, f32[3,64,512]{2,1,0:T(8,128)} %bitcast.6, bf16[384,192]{1,0:T(8,128)(2,1)} %constant.12.clone.left_hbm, bf16[384,640]{1,0:T(8,128)(2,1)} %constant.13.clone.right_hbm, f32[2,64,512]{2,1,0:T(8,128)} %constant.14.clone.fields_hbm, ...), custom_call_target="tpu_custom_call" | custom-call | tf_op jit(solution)/shard_map/pallas_call | solution.py:533
  66.4 1.1 %slice_bitcast_fusion = f32[21]{0:T(128)} fusion(f32[1,128]{1,0:T(1,128)} %get-tuple-element.5), kind=kLoop, calls=%fused_computation | loop fusion | bytes 168 | tf_op jit(solution)/shard_map/squeeze | solution.py:577
  67.5 1.8 %copy.11 = f32[3,8,8,512]{3,2,1,0:T(8,128)} copy(f32[3,8,8,512]{3,2,1,0:T(8,128)} %bitcast.7) | data formatting | bytes 786432

commit v3 on v1

--- a/solution.py
+++ b/solution.py
@@ -163,7 +163,7 @@
 def kernel(
     count_x, count_y, size_b, size_z,
     basis_hbm, base_hbm, left_hbm, right_hbm, fields_hbm, down_hbm, up_hbm, spread_hbm,
-    out, hess,
+    out, hess, norm,
     basis, base, left, right, fields, down, up, slopes, spread, field, star, phi, source, state,
     xs3, ys3, cs3, xr3, yr3, cr3,
     xs1, ys1, cs1, xr1, yr1, cr1,
@@ -192,9 +192,6 @@
     ]
     for pos in (0, 1, 4, 5, 2, 6, 7, 8):
         loads[pos].start()
-    for buffer in (xr3, yr3, cr3, xr1, yr1, cr1, coarse_r):
-        buffer[...] = jnp.zeros_like(buffer)
-
     barrier = pltpu.get_barrier_semaphore()
 
     def greet(step, carry):
@@ -214,6 +211,24 @@
         if dy:
             tests.append((gy > 0) if dy < 0 else (gy < count_y - 1))
         return tests[0] if len(tests) == 1 else tests[0] & tests[1]
+
+    def clear(ref):
+        ref[...] = jnp.zeros(ref.shape, ref.dtype)
+
+    for dx, dy in DIRS:
+        ox, oy = (dx + 1) // 2, (dy + 1) // 2
+
+        @pl.when(jnp.logical_not(there(dx, dy)))
+        def _():
+            for xr, yr, cr in ((xr3, yr3, cr3), (xr1, yr1, cr1)):
+                if dy == 0:
+                    clear(xr.at[:, ox])
+                elif dx == 0:
+                    clear(yr.at[:, oy])
+                else:
+                    clear(cr.at[:, 2 * ox + oy])
+            if dy == 0:
+                clear(coarse_r.at[:, 2 * ox])
 
     row = lax.broadcasted_iota(jnp.int32, (64, size_z), 0)
     lane = lax.broadcasted_iota(jnp.int32, (64, size_z), 1)
@@ -433,11 +448,10 @@
     pressure = phi[...]
     both = by_left(0, 128, pressure)
     send([both[:64], both[64:], by_right(0, 1, pressure)[0]], 2, True)
+    source[...] = weight_3[...] * rmult * (1.0 / (8.0 * total * (size_z // 8)))
+    loads[3].wait()
     for c, value in enumerate(receive(3, 2, True)):
         star[c] = star[c] - value * rmult
-    loads[3].wait()
-    mass = weight_3[...] * rmult * (1.0 / (8.0 * total * (size_z // 8)))
-    phi[...] = mass
 
     def fold(value):
         return functools.reduce(
@@ -447,7 +461,7 @@
     def products_of(step, sums):
         c, x = step // 8, lax.rem(step, 8)
         rows = pl.ds(pl.multiple_of(8 * x, 8), 8)
-        weighted = star[c, rows, :] * phi[rows, :]
+        weighted = star[c, rows, :] * source[rows, :]
         return tuple(
             total_k + fold(basis[k, c, rows, :] * weighted) for k, total_k in enumerate(sums)
         )
@@ -470,8 +484,17 @@
 
         lax.fori_loop(1, total, to, 0)
         red_r[which, me] = value
+        if which == 0:
+            for round_idx in range(2 * SWEEPS):
+                each_copy(round_idx, False, "sent")
+        else:
+            for round_idx in range(3):
+                each_copy(round_idx, True, "sent")
+            for sweep in range(SWEEPS):
+                coarse_wait(sweep, csend)
         part = red_r.at[which, pl.ds(0, total - 1)]
         pltpu.make_async_copy(part, part, rrecv.at[which]).wait()
+        pltpu.make_async_copy(part, part, rsend.at[which]).wait()
         return functools.reduce(lambda a, b: a + b, [red_r[which, j] for j in range(total)])
 
     own = jnp.zeros((1, 128), jnp.float32)
@@ -495,27 +518,18 @@
             for k in range(size_b):
                 value = value - spreads[k] * basis[k, c, rows, lanes]
             star[c, rows, lanes] = value
-            squares = squares + value * value * phi[rows, lanes]
+            squares = squares + value * value * source[rows, lanes]
         return squares
 
     squares = lax.fori_loop(0, 24, remainder_of, zero)
+    store = pltpu.make_async_copy(star, out, load_sem.at[9])
+    store.start()
     squared = jnp.sum(jnp.sum(squares, axis=0, keepdims=True), axis=1, keepdims=True)
     squared = all_sum(1, jnp.broadcast_to(squared, (1, 128)))
     beta = jnp.sqrt(squared + norm_eps)
     hess[...] = jnp.where(lane_1 == size_b, beta, hcol)
-    scale = 1.0 / beta[:, 0:1]
-    for c in range(3):
-        out[c] = star[c] * scale
-
-    for round_idx in range(3):
-        each_copy(round_idx, True, "sent")
-    for round_idx in range(2 * SWEEPS):
-        each_copy(round_idx, False, "sent")
-    for sweep in range(SWEEPS):
-        coarse_wait(sweep, csend)
-    for which in range(2):
-        part = red_r.at[which, pl.ds(0, total - 1)]
-        pltpu.make_async_copy(part, part, rsend.at[which]).wait()
+    norm[...] = jnp.broadcast_to(beta[:, 0:1], norm.shape)
+    store.wait()
 
 
 def per_device(basis, base_flow):
@@ -537,14 +551,15 @@
         exchange += [vmem(shape) for shape in shapes * 2]
     spec_v = pl.BlockSpec(memory_space=pltpu.VMEM)
     spec_any = pl.BlockSpec(memory_space=pl.ANY)
-    out, hess = pl.pallas_call(
+    out, hess, norm = pl.pallas_call(
         functools.partial(kernel, count_x, count_y, size_b, size_z),
         out_shape=(
             jax.ShapeDtypeStruct((3, 64, size_z), jnp.float32),
             jax.ShapeDtypeStruct((1, 128), jnp.float32),
+            jax.ShapeDtypeStruct((1, size_z), jnp.float32),
         ),
         in_specs=[spec_any] * 8,
-        out_specs=(spec_v, spec_v),
+        out_specs=(spec_any, spec_v, spec_v),
         scratch_shapes=[
             vmem((size_b, 3, 64, size_z)),
             vmem((3, 64, size_z)),
@@ -565,7 +580,7 @@
             vmem((SWEEPS, 3, count_y, 1, lanes)),
             vmem((2, 1, 128)),
             vmem((2, count_x * count_y, 1, 128)),
-            dma((9,)),
+            dma((10,)),
             dma((3, 8)),
             dma((3, 8)),
             dma((2 * SWEEPS, 8)),
@@ -583,7 +598,7 @@
         base_flow.reshape(3, 64, size_z),
         *[jnp.asarray(table) for table in tables],
     )
-    return (out.reshape(base_flow.shape), hess[0, : size_b + 1])
+    return (out.reshape(base_flow.shape) / norm[0], hess[0, : size_b + 1])
 
 
 def solution(mesh):

time: 68.6 us -> 68.3 us (level)
  other arithmetic: 0 us -> 1.8 us
  local copies, waits for them, and re-layouts: 2.89 us -> 1.19 us
    div x0 -> x1, other arithmetic: none -> 1.8 us  [per_device(): return (out.reshape(base_flow.shape) / norm[0], hess[0, :size_b + 1])]
    unnamed x1 -> x0, local copies, waits for them, and re-layouts: 1.77 us -> none
where the time goes in v3:
time: 68.3 us; the launch traced here: 68.1 us
  Pallas kernels  64.5 us (94%)
  other arithmetic  1.8 us (3%)
  local copies, waits for them, and re-layouts  1.19 us (2%)
    pallas_call x1, Pallas kernels, per_device(): pl.pallas_call(functools.partial(kernel, count_x, count_y, size_b, size_z...  64.5 us
    div x1, other arithmetic, per_device(): return (out.reshape(base_flow.shape) / norm[0], hess[0, :size_b + 1])  1.8 us

profile of v3, /device:TPU:0, one launch (start us, length us, event | category | flops | bytes accessed | tf_op | source)
XLA Modules:
  0.0 68.1 jit_solution(10396726178289573941)
XLA Ops:
  0.6 64.5 %shard_map.95 = (f32[3,64,512]{2,1,0:T(8,128)}, f32[1,128]{1,0:T(1,128)}, f32[1,512]{1,0:T(1,128)}) custom-call(f32[20,3,64,512]{3,2,1,0:T(8,128)} %bitcast.7, f32[3,64,512]{2,1,0:T(8,128)} %bitcast.8, bf16[384,192]{1,0:T(8,128)(2,1)} %constant.12.clone.left_hbm, bf16[384,640]{1,0:T(8,128)(2,1)} %constant.13.clone.right_hbm, ...), custom_call_target="tpu_custom_call" | custom-call | tf_op jit(solution)/shard_map/pallas_call | solution.py:554
  65.1 1.8 %bitcast_divide_fusion = f32[3,8,8,512]{3,2,1,0:T(8,128)} fusion(f32[3,64,512]{2,1,0:T(8,128)} %get-tuple-element.5, f32[512]{0:T(512)} %bitcast.9), kind=kLoop, calls=%fused_computation | loop fusion | flops 98304 | bytes 788480 | tf_op jit(solution)/shard_map/div | solution.py:601
  66.9 1.2 %slice_bitcast_fusion = f32[21]{0:T(128)} fusion(f32[1,128]{1,0:T(1,128)} %get-tuple-element.7), kind=kLoop, calls=%fused_computation.1 | loop fusion | bytes 168 | tf_op jit(solution)/shard_map/squeeze | solution.py:601

commit v4 on v3

--- a/solution.py
+++ b/solution.py
@@ -387,11 +387,11 @@
                 return carry
 
             if dx == 0:
-                lax.fori_loop(1, count_y, to, 0)
+                lax.fori_loop(1, count_y, to, 0, unroll=True)
             else:
                 @pl.when(there(dx, 0))
                 def _():
-                    lax.fori_loop(0, count_y, to, 0)
+                    lax.fori_loop(0, count_y, to, 0, unroll=True)
 
     def coarse_wait(sweep, sems):
         for pos, dx in enumerate((-1, 0, 1)):

time: 68.3 us -> 67.2 us (0.984)
  Pallas kernels: 64.5 us -> 63.4 us
    pallas_call x1, Pallas kernels: 64.5 us -> 63.4 us  [per_device(): pl.pallas_call(functools.partial(kernel, count_x, count_y, size_b, size_z...]
where the time goes in v4:
time: 67.2 us; the launch traced here: 67.1 us
  Pallas kernels  63.4 us (94%)
  other arithmetic  1.8 us (3%)
  local copies, waits for them, and re-layouts  1.19 us (2%)
    pallas_call x1, Pallas kernels, per_device(): pl.pallas_call(functools.partial(kernel, count_x, count_y, size_b, size_z...  63.4 us
    div x1, other arithmetic, per_device(): return (out.reshape(base_flow.shape) / norm[0], hess[0, :size_b + 1])  1.8 us

profile of v4, /device:TPU:0, one launch (start us, length us, event | category | flops | bytes accessed | tf_op | source)
XLA Modules:
  0.0 67.1 jit_solution(1038009605956087030)
XLA Ops:
  0.6 63.4 %shard_map.95 = (f32[3,64,512]{2,1,0:T(8,128)}, f32[1,128]{1,0:T(1,128)}, f32[1,512]{1,0:T(1,128)}) custom-call(f32[20,3,64,512]{3,2,1,0:T(8,128)} %bitcast.7, f32[3,64,512]{2,1,0:T(8,128)} %bitcast.8, bf16[384,192]{1,0:T(8,128)(2,1)} %constant.12.clone.left_hbm, bf16[384,640]{1,0:T(8,128)(2,1)} %constant.13.clone.right_hbm, ...), custom_call_target="tpu_custom_call" | custom-call | tf_op jit(solution)/shard_map/pallas_call | solution.py:554
  64.1 1.8 %bitcast_divide_fusion = f32[3,8,8,512]{3,2,1,0:T(8,128)} fusion(f32[3,64,512]{2,1,0:T(8,128)} %get-tuple-element.5, f32[512]{0:T(512)} %bitcast.9), kind=kLoop, calls=%fused_computation | loop fusion | flops 98304 | bytes 788480 | tf_op jit(solution)/shard_map/div | solution.py:601
  65.9 1.2 %slice_bitcast_fusion = f32[21]{0:T(128)} fusion(f32[1,128]{1,0:T(1,128)} %get-tuple-element.7), kind=kLoop, calls=%fused_computation.1 | loop fusion | bytes 168 | tf_op jit(solution)/shard_map/squeeze | solution.py:601
